TPU v7x, 32 devices: a whole 2x2x4 slice. The times are simulated.
32 devices in a mesh: groups: 2 (over y), dp: 16 (over z, x, core).
Axes of the slice: x: 2, y: 2, z: 4, core: 2. Of those that a mesh axis runs over, the one named last changes fastest.
Arguments:
- particles: bfloat16 [2048, 128, 128], P(('groups', 'dp')), parts along dimension 0, may hold values from -20 to 20
- refs: bfloat16 [128, 256, 128], P('dp', 'groups'), parts along dimension 1, may hold values from -0.5 to 0.5
- ctf_group: int32 [2048], P(('groups', 'dp')), parts along dimension 0, may hold values from 0 to 31, as said below
- defocus: float32 [64], P('groups'), parts along dimension 0, may hold values from 0.5 to 2
- class_prior: float32 [256], P('groups'), parts along dimension 0, may hold values from 0.25 to 4
- cycle_weight: float32 [64], replicated, may hold values from 0.5 to 2
Outputs:
- new_refs: float32 [128, 256, 128], P('dp', 'groups'), parts along dimension 1
- log_evidence: float32 [2048], P(('groups', 'dp')), parts along dimension 0
There are 2 independent parts, one for each index of `groups`. A program takes and returns all parts, laid end to end along the dimension named above; an argument that names none is the same for every part. Nothing has to cross between parts.
Inputs may be any that keep to these rules, and one draw needn't show every extreme that they name: `ctf_group`: CTF groups follow the particle order: particle n belongs to group n * 32 // 1024 or the next one, capped at 31.
All inputs are finite; a program needn't handle non-finite values.
Results may differ from a plain program's by a relative error of at most 0.0045.
Values may be sent and summed in bfloat16 or wider, within the bound.
A program may use at most 64 MiB of HBM per device.

v0:
```python
import math
import jax
import jax.numpy as jnp
from jax import lax
from jax.sharding import PartitionSpec as P

M = 128
R = 64
ROT = 36
G = 32


def ctf_table(defocus):
    radius = (jnp.arange(R, dtype=jnp.float32) + 1.0) / R
    phase = 20.0 * defocus[:, None] * radius[None, :] ** 2
    return -(0.995 * jnp.sin(phase) + 0.1 * jnp.cos(phase))


def angle_tables():
    harmonic = jnp.arange(M, dtype=jnp.float32)[:, None]
    turning = jnp.arange(ROT, dtype=jnp.float32)[None, :]
    theta = 2.0 * math.pi * harmonic * turning / ROT
    return (jnp.cos(theta), jnp.sin(theta))


def shards(particles, refs, ctf_group, defocus, class_prior, cycle_weight):
    highest = lax.Precision.HIGHEST
    ctf = ctf_table(defocus)
    cos_table, sin_table = angle_tables()
    onehot = (ctf_group[:, None] == jnp.arange(G, dtype=jnp.int32)[None, :]).astype(jnp.float32)
    gain_table = jnp.concatenate([cycle_weight[None, :] * ctf, cycle_weight[None, :] * ctf], axis=1)
    gain = jnp.dot(onehot, gain_table, precision=highest)
    weighted = (particles.astype(jnp.float32) * gain[:, None, :]).astype(jnp.bfloat16)
    turned = jnp.concatenate([weighted[:, :, R:], -weighted[:, :, :R]], axis=2)
    all_refs = lax.all_gather(refs, "dp", axis=0, tiled=True)
    part_weighted = weighted
    part_turned = turned
    part_cos = cos_table
    part_sin = sin_table
    cross_real = jnp.einsum(
        "nmq,mkq->mnk", part_weighted, all_refs, preferred_element_type=jnp.float32
    )
    cross_imag = jnp.einsum(
        "nmq,mkq->mnk", part_turned, all_refs, preferred_element_type=jnp.float32
    )
    corr = jnp.einsum("mnk,mj->jnk", cross_real, part_cos, precision=highest)
    corr = corr - jnp.einsum("mnk,mj->jnk", cross_imag, part_sin, precision=highest)
    wide_refs = all_refs.astype(jnp.float32)
    energy = jnp.sum(wide_refs[:, :, :R] ** 2 + wide_refs[:, :, R:] ** 2, axis=0)
    corr, energy = (corr, energy)
    quadratic = jnp.dot(cycle_weight[None, :] * ctf * ctf, energy.T, precision=highest)
    norm_term = jnp.dot(onehot, quadratic, precision=highest)
    scores = corr - 0.5 * norm_term[None, :, :] + jnp.log(class_prior)[None, None, :]
    top = jnp.max(scores, axis=(0, 2), keepdims=True)
    expo = jnp.exp(scores - top)
    total = jnp.sum(expo, axis=(0, 2), keepdims=True)
    posterior = expo / total
    log_evidence = top[0, :, 0] + jnp.log(total[0, :, 0])
    local_mass = jnp.dot(onehot.T, jnp.sum(posterior, axis=0), precision=highest)
    mass = lax.psum(local_mass, "dp")
    part_cos = cos_table
    part_sin = sin_table
    post_real = jnp.einsum("jnk,mj->mnk", posterior, part_cos, precision=highest).astype(
        jnp.bfloat16
    )
    post_imag = jnp.einsum("jnk,mj->mnk", posterior, part_sin, precision=highest).astype(
        jnp.bfloat16
    )
    part_weighted = weighted
    part_turned = turned
    term = jnp.einsum("mnk,nmq->mkq", post_real, part_weighted, preferred_element_type=jnp.float32)
    numer = lax.psum_scatter(
        term
        - jnp.einsum("mnk,nmq->mkq", post_imag, part_turned, preferred_element_type=jnp.float32),
        "dp",
        scatter_dimension=0,
        tiled=True,
    )
    denom = 1.0 + jnp.dot(mass.T, cycle_weight[None, :] * ctf * ctf, precision=highest)
    denom_wide = jnp.concatenate([denom, denom], axis=1)
    new_refs = numer / denom_wide[None, :, :]
    return (new_refs, log_evidence)


def solution(mesh):
    in_specs = (
        P(("groups", "dp"), None, None),
        P("dp", "groups", None),
        P(("groups", "dp")),
        P("groups"),
        P("groups"),
        P(),
    )
    out_specs = (P("dp", "groups", None), P(("groups", "dp")))
    return jax.shard_map(shards, mesh=mesh, in_specs=in_specs, out_specs=out_specs, check_vma=False)
```

profile of v0, /device:TPU:0, one launch (start us, length us, event | category | flops | bytes accessed | tf_op | source)
XLA Modules:
  0.0 214.6 jit_solution(5967293046546979658)
XLA Ops:
  7.2 0.7 all-gather.2.cloned.1.call-update
  7.9 0.7 log.6
  8.6 0.7 broadcast_multiply_fusion
  9.3 0.8 fusion.38
  10.1 0.9 fusion.20
  11.0 2.9 %multiply_convert_fusion = bf16[64,128,128]{2,0,1:T(8,128)(2,1)S(1)} fusion(bf16[64,128,128]{2,1,0:T(8,128)(2,1)} %param.6, f32[64,128]{1,0:T(8,128)S(1)} %fusion.20), kind=kLoop, calls=%fused_computation.10 | loop fusion | flops 3145728 | bytes 4227072 | tf_op jit(solution)/shard_map/convert_element_type | solution.py:33
  13.9 2.7 %fusion.70 = (bf16[64,128,64]{2,0,1:T(8,128)(2,1)}, bf16[64,128,64]{2,0,1:T(8,128)(2,1)}) fusion(bf16[64,128,128]{2,0,1:T(8,128)(2,1)S(1)} %multiply_convert_fusion), kind=kLoop, calls=%fused_computation.77 | loop fusion | flops 524288 | bytes 4194304 | tf_op jit(solution)/shard_map/slice | solution.py:34
  16.6 46.6 %all-gather.2.cloned.1.call-done = bf16[128,128,128]{2,1,0:T(8,128)(2,1)} async-done(((bf16[8,128,128]{2,1,0:T(8,128)(2,1)}), bf16[128,128,128]{2,1,0:T(8,128)(2,1)}) %all-gather.2.cloned.1.call-update) | async-done | bytes 4194320 | tf_op jit(solution)/shard_map/all_gather | solution.py:35
  63.3 3.2 %convert_element_type.18 = f32[128,128,128]{2,1,0:T(8,128)S(1)} convert(bf16[128,128,128]{2,1,0:T(8,128)(2,1)} %all-gather.2.cloned.1.call-done) | non-fusion elementwise | flops 2097152 | bytes 12582912 | tf_op jit(solution)/shard_map/convert_element_type | solution.py:48
  66.6 2.5 %fusion.1 = f32[128,64]{1,0:T(8,128)S(1)} fusion(f32[128,128,128]{2,1,0:T(8,128)S(1)} %convert_element_type.18), kind=kLoop, calls=%fused_computation.2 | loop fusion | flops 4186112 | bytes 8421376 | tf_op jit(solution)/shard_map/reduce_sum | solution.py:49
  70.0 3.0 %fusion.18 = f32[128,64,128]{2,1,0:T(8,128)S(1)} fusion(bf16[128,128,128]{2,1,0:T(8,128)(2,1)S(1)} %copy-done, bf16[64,128,64]{2,0,1:T(8,128)(2,1)S(1)} %copy-done.2, bf16[64,128,64]{2,0,1:T(8,128)(2,1)S(1)} %copy-done.1), kind=kOutput, calls=%fused_computation.23 | convolution fusion | flops 272629760 | bytes 10485760 | tf_op jit(solution)/shard_map/nmq,mkq->mnk/dot_general | solution.py:43
  73.0 4.7 %fusion.2 = f32[36,64,128]{2,0,1:T(8,128)S(1)} fusion(f32[128,64,128]{2,1,0:T(8,128)S(1)} %fusion.18, f32[128]{0:T(128)S(1)} %iota_multiply_fusion), kind=kOutput, calls=%fused_computation.6 | convolution fusion | flops 452994048 | bytes 5374464 | tf_op jit(solution)/shard_map/mnk,mj->jnk/dot_general | solution.py:47
  77.7 3.0 %fusion.72 = f32[128,64,128]{2,1,0:T(8,128)S(1)} fusion(bf16[64,128,128]{2,0,1:T(8,128)(2,1)S(1)} %multiply_convert_fusion, bf16[128,128,128]{2,1,0:T(8,128)(2,1)S(1)} %copy-done), kind=kOutput, calls=%fused_computation.79 | convolution fusion | flops 268435456 | bytes 10485760 | tf_op jit(solution)/shard_map/nmq,mkq->mnk/dot_general | solution.py:40
  80.6 5.3 %fusion.71 = (f32[64]{0:T(128)S(1)}, f32[36,64,128]{2,0,1:T(8,128)S(1)}) fusion(f32[128]{0:T(128)S(1)} %log.6, f32[64,128]{1,0:T(8,128)S(1)} %convolution_multiply_fusion, f32[36,64,128]{2,0,1:T(8,128)S(1)} %fusion.2, f32[128,64,128]{2,1,0:T(8,128)S(1)} %fusion.72, f32[128]{0:T(128)S(1)} %iota_multiply_fusion), kind=kOutput, calls=%fused_computation.78 | convolution fusion | flops 454173632 | bytes 6587648 | tf_op jit(solution)/shard_map/mnk,mj->jnk/dot_general | solution.py:46
  85.9 1.0 fusion.17
  86.9 3.9 %fusion.24 = bf16[128,64,128]{2,0,1:T(8,128)(2,1)S(1)} fusion(f32[128]{0:T(128)S(1)} %iota_multiply_fusion, f32[36,64,128]{2,0,1:T(8,128)S(1)} %get-tuple-element.5, f32[64]{0:T(128)S(1)} %fusion.17, f32[64]{0:T(128)S(1)} %get-tuple-element.4), kind=kOutput, calls=%fused_computation.34 | convolution fusion | flops 453583872 | bytes 3277824 | tf_op jit(solution)/shard_map/jnk,mj->mnk/dot_general | solution.py:63
  90.8 3.9 %fusion.21 = bf16[128,64,128]{2,0,1:T(8,128)(2,1)S(1)} fusion(f32[128]{0:T(128)S(1)} %iota_multiply_fusion, f32[36,64,128]{2,0,1:T(8,128)S(1)} %get-tuple-element.5, f32[64]{0:T(128)S(1)} %fusion.17, f32[64]{0:T(128)S(1)} %get-tuple-element.4), kind=kOutput, calls=%fused_computation.31 | convolution fusion | flops 453583872 | bytes 3277824 | tf_op jit(solution)/shard_map/jnk,mj->mnk/dot_general | solution.py:66
  94.7 2.0 fusion.6
  96.7 6.8 %convolution_subtract_fusion = f32[128,128,128]{2,1,0:T(8,128)} fusion(f32[128,128,128]{2,1,0:T(8,128)S(1)} %fusion.6, bf16[128,64,128]{2,0,1:T(8,128)(2,1)S(1)} %fusion.21, bf16[64,128,64]{2,0,1:T(8,128)(2,1)S(1)} %copy-done.2, bf16[64,128,64]{2,0,1:T(8,128)(2,1)S(1)} %copy-done.1), kind=kOutput, calls=%fused_computation.11 | convolution fusion | flops 274726912 | bytes 20971520 | tf_op jit(solution)/shard_map/mnk,nmq->mkq/dot_general | solution.py:74
  104.1 61.6 %psum.7 = f32[32,128]{1,0:T(8,128)S(1)} all-reduce(f32[32,128]{1,0:T(8,128)S(1)} %fusion.19), channel_id=1, replica_groups=mesh['groups'=2,'dp'=16] {'dp'}, use_global_device_ids=true, to_apply=%region_5.0 | all-reduce | flops 4096 | bytes 32768 | tf_op jit(solution)/shard_map/psum | solution.py:60
  165.7 0.4 convolution_add_fusion
  166.2 0.5 log_add_fusion
  166.8 39.1 %reduce-scatter.2.cloned.1.call-done = f32[8,128,128]{2,1,0:T(8,128)} async-done(((f32[128,128,128]{2,1,0:T(8,128)}), f32[8,128,128]{2,1,0:T(8,128)}) %reduce-scatter.2.cloned.1.call-update) | async-done | bytes 524304 | tf_op jit(solution)/shard_map/reduce_scatter | solution.py:72
  205.9 1.9 broadcast_divide_fusion
  (21 shorter events, 1.7 us)
Async XLA Ops:
  7.2 56.1 %all-gather.2.cloned.1.call-start = ((), (), s32[]{:S(2)}) async-start(), calls=%async_computation.1 | async-start | bytes 4456448 | tf_op jit(solution)/shard_map/all_gather | solution.py:35
  7.9 198.0 %reduce-scatter.2.cloned.1.call-start = ((), (), s32[]{:S(2)}) async-start(), calls=%async_computation.2 | async-start | bytes 8912896 | tf_op jit(solution)/shard_map/reduce_scatter | solution.py:72
  66.5 2.6 %copy-start.3 = (f32[64]{0:T(128)S(1)}, f32[64]{0:T(128)}, u32[]{:S(2)}) copy-start(f32[64]{0:T(128)} %param.11) | copy-start | bytes 772
  66.5 2.9 %copy-start.4 = (s32[64]{0:T(128)S(1)}, s32[64]{0:T(128)}, u32[]{:S(2)}) copy-start(s32[64]{0:T(128)} %param.8) | copy-start | bytes 772
  66.5 3.1 %copy-start = (bf16[128,128,128]{2,1,0:T(8,128)(2,1)S(1)}, bf16[128,128,128]{2,1,0:T(8,128)(2,1)}, u32[]{:S(2)}) copy-start(bf16[128,128,128]{2,1,0:T(8,128)(2,1)} %all-gather.2.cloned.1.call-done) | copy-start | bytes 12582916
  66.5 3.1 %copy-start.1 = (bf16[64,128,64]{2,0,1:T(8,128)(2,1)S(1)}, bf16[64,128,64]{2,0,1:T(8,128)(2,1)}, u32[]{:S(2)}) copy-start(bf16[64,128,64]{2,0,1:T(8,128)(2,1)} %get-tuple-element.2) | copy-start | bytes 3145732
  66.5 3.5 %copy-start.2 = (bf16[64,128,64]{2,0,1:T(8,128)(2,1)S(1)}, bf16[64,128,64]{2,0,1:T(8,128)(2,1)}, u32[]{:S(2)}) copy-start(bf16[64,128,64]{2,0,1:T(8,128)(2,1)} %get-tuple-element.3) | copy-start | bytes 3145732
Sparse Core Ops, SparseCore 0:
  10.1 53.0 all-gather.1
  103.6 102.2 reduce-scatter.1
where the time goes:
time: 215 us
  waiting for transfers between devices  86.5 us (40%)
  blocking collectives  61.6 us (29%)
  matrix products  34.5 us (16%)
  other arithmetic  16.6 us (8%)
  between operations  14.2 us (7%)
    psum x1, blocking collectives, shards(): mass = lax.psum(local_mass, 'dp')  61.6 us
    all_gather x1, waiting for transfers between devices, shards(): all_refs = lax.all_gather(refs, 'dp', axis=0, tiled=True)  46.6 us
    reduce_scatter x1, waiting for transfers between devices, shards(): lax.psum_scatter(term - jnp.einsum('mnk,nmq->mkq', post_imag, part_turned...  39.1 us
    dot_general x1, matrix products, shards(): jnp.einsum('mnk,nmq->mkq', post_imag, part_turned, preferred_element_type...  6.76 us
    dot_general x1, matrix products, shards(): corr = jnp.einsum('mnk,mj->jnk', cross_real, part_cos, precision=highest)  5.3 us
    dot_general x1, matrix products, shards(): jnp.einsum('mnk,mj->jnk', cross_imag, part_sin, precision=highest)  4.69 us
  transfers between devices with their start and end apart: 2, of which 2 were waited for; matrix products, arithmetic and copies ran while one was open for 5% of the time, Pallas kernels for 0%

commit v1 on v0

--- a/solution.py
+++ b/solution.py
@@ -32,7 +32,9 @@
     gain = jnp.dot(onehot, gain_table, precision=highest)
     weighted = (particles.astype(jnp.float32) * gain[:, None, :]).astype(jnp.bfloat16)
     turned = jnp.concatenate([weighted[:, :, R:], -weighted[:, :, :R]], axis=2)
-    all_refs = lax.all_gather(refs, "dp", axis=0, tiled=True)
+    all_refs = jnp.concatenate(
+        lax.all_to_all(jnp.stack([refs] * lax.axis_size("dp")), "dp", 0, 0), axis=0
+    )
     part_weighted = weighted
     part_turned = turned
     part_cos = cos_table

time: 215 us -> 263 us (1.22)
  waiting for transfers between devices: 86.5 us -> 110 us
  blocking collectives: 61.6 us -> 78.1 us
  starting transfers between devices: 0.08 us -> 7.62 us
  local copies, waits for them, and re-layouts: 1.12 us -> 4.28 us
  other arithmetic: 16.6 us -> 13.5 us
    all_to_all x0 -> x1, waiting for transfers between devices: none -> 71.4 us  [shards(): lax.all_to_all(jnp.stack([refs] * lax.axis_size('dp')), 'dp', 0, 0)]
    all_gather x1 -> x0, waiting for transfers between devices: 46.6 us -> none  [shards(): all_refs = lax.all_gather(refs, 'dp', axis=0, tiled=True)]
    psum x1, blocking collectives: 61.6 us -> 78.1 us  [shards(): mass = lax.psum(local_mass, 'dp')]
    all_to_all x0 -> x1, starting transfers between devices: none -> 7.58 us  [shards(): lax.all_to_all(jnp.stack([refs] * lax.axis_size('dp')), 'dp', 0, 0)]
    another operation x0 -> x1, local copies, waits for them, and re-layouts: none -> 3.05 us  [shards(): jnp.stack([refs] * lax.axis_size('dp'))]
  transfers between devices with their start and end apart: 2 -> 2, of which waited for: 2 -> 2; matrix products, arithmetic and copies ran while one was open for 5% -> 3% of each run, Pallas kernels for 0% -> 0%
where the time goes in v1:
time: 263 us
  waiting for transfers between devices  110 us (42%)
  blocking collectives  78.1 us (30%)
  matrix products  34.8 us (13%)
  between operations  14.2 us (5%)
  other arithmetic  13.5 us (5%)
  starting transfers between devices  7.62 us (3%)
  local copies, waits for them, and re-layouts  4.28 us (2%)
    psum x1, blocking collectives, shards(): mass = lax.psum(local_mass, 'dp')  78.1 us
    all_to_all x1, waiting for transfers between devices, shards(): lax.all_to_all(jnp.stack([refs] * lax.axis_size('dp')), 'dp', 0, 0)  71.4 us
    reduce_scatter x1, waiting for transfers between devices, shards(): lax.psum_scatter(term - jnp.einsum('mnk,nmq->mkq', post_imag, part_turned...  39.1 us
    all_to_all x1, starting transfers between devices, shards(): lax.all_to_all(jnp.stack([refs] * lax.axis_size('dp')), 'dp', 0, 0)  7.58 us
    dot_general x1, matrix products, shards(): jnp.einsum('mnk,nmq->mkq', post_imag, part_turned, preferred_element_type...  6.76 us
  transfers between devices with their start and end apart: 2, of which 2 were waited for; matrix products, arithmetic and copies ran while one was open for 3% of the time, Pallas kernels for 0%

profile of v1, /device:TPU:0, one launch (start us, length us, event | category | flops | bytes accessed | tf_op | source)
XLA Modules:
  0.0 263.1 jit_solution(4533943736717276272)
XLA Ops:
  7.2 1.1 copy.11
  8.3 3.0 %stack.2 = bf16[16,8,128,128]{2,3,1,0:T(8,128)(2,1)} broadcast(bf16[8,128,128]{1,2,0:T(8,128)(2,1)S(1)} %copy.11), dimensions={1,2,3} | broadcast | bytes 4456448 | tf_op jit(solution)/shard_map/stack | solution.py:36
  11.3 7.6 %all-to-all-start = ((bf16[16,8,128,128]{2,3,1,0:T(8,128)(2,1)}), bf16[16,8,128,128]{2,3,1,0:T(8,128)(2,1)}, u32[]{:S(2)}, u32[]{:S(2)}) async-start(bf16[16,8,128,128]{2,3,1,0:T(8,128)(2,1)} %stack.2), calls=%async_computation | async-start | bytes 8388608 | tf_op jit(solution)/shard_map/all_to_all | solution.py:36
  19.4 2.9 %multiply_convert_fusion = bf16[64,128,128]{2,0,1:T(8,128)(2,1)S(1)} fusion(bf16[64,128,128]{2,1,0:T(8,128)(2,1)} %param.6, f32[64,128]{1,0:T(8,128)S(1)} %fusion.20), kind=kLoop, calls=%fused_computation.10 | loop fusion | flops 3145728 | bytes 4227072 | tf_op jit(solution)/shard_map/convert_element_type | solution.py:33
  22.4 2.7 %fusion.70 = (bf16[64,128,64]{2,0,1:T(8,128)(2,1)}, bf16[64,128,64]{2,0,1:T(8,128)(2,1)}) fusion(bf16[64,128,128]{2,0,1:T(8,128)(2,1)S(1)} %multiply_convert_fusion), kind=kLoop, calls=%fused_computation.78 | loop fusion | flops 524288 | bytes 4194304 | tf_op jit(solution)/shard_map/slice | solution.py:34
  25.1 71.4 %all-to-all-done = bf16[16,8,128,128]{2,3,1,0:T(8,128)(2,1)} async-done(((bf16[16,8,128,128]{2,3,1,0:T(8,128)(2,1)}), bf16[16,8,128,128]{2,3,1,0:T(8,128)(2,1)}, u32[]{:S(2)}, u32[]{:S(2)}) %all-to-all-start) | async-done | bytes 4194336 | tf_op jit(solution)/shard_map/all_to_all | solution.py:36
  96.5 3.3 %bitcast_convert_fusion = f32[128,128,128]{1,2,0:T(8,128)S(1)} fusion(bf16[16,8,128,128]{2,3,1,0:T(8,128)(2,1)} %all-to-all-done), kind=kLoop, calls=%fused_computation.67 | loop fusion | flops 2097152 | bytes 12582912 | tf_op jit(solution)/shard_map/convert_element_type | solution.py:50
  99.7 0.6 fusion.1
  100.4 0.3 fusion.54
  100.9 3.6 %fusion.72 = f32[128,64,128]{2,1,0:T(8,128)S(1)} fusion(bf16[64,128,128]{2,0,1:T(8,128)(2,1)S(1)} %multiply_convert_fusion, bf16[128,128,128]{1,2,0:T(8,128)(2,1)} %bitcast.1), kind=kOutput, calls=%fused_computation.80 | convolution fusion | flops 268435456 | bytes 10485760 | tf_op jit(solution)/shard_map/nmq,mkq->mnk/dot_general | solution.py:42
  104.5 3.5 %fusion.18 = f32[128,64,128]{2,1,0:T(8,128)S(1)} fusion(bf16[128,128,128]{1,2,0:T(8,128)(2,1)} %bitcast.1, bf16[64,128,64]{2,0,1:T(8,128)(2,1)S(1)} %copy-done.1, bf16[64,128,64]{2,0,1:T(8,128)(2,1)S(1)} %copy-done), kind=kOutput, calls=%fused_computation.23 | convolution fusion | flops 272629760 | bytes 10485760 | tf_op jit(solution)/shard_map/nmq,mkq->mnk/dot_general | solution.py:45
  108.0 4.7 %fusion.2 = f32[36,64,128]{2,0,1:T(8,128)S(1)} fusion(f32[128,64,128]{2,1,0:T(8,128)S(1)} %fusion.18, f32[128]{0:T(128)S(1)} %iota_multiply_fusion), kind=kOutput, calls=%fused_computation.6 | convolution fusion | flops 452994048 | bytes 5374464 | tf_op jit(solution)/shard_map/mnk,mj->jnk/dot_general | solution.py:49
  112.7 5.2 %fusion.71 = (f32[64]{0:T(128)S(1)}, f32[36,64,128]{2,0,1:T(8,128)S(1)}) fusion(f32[128]{0:T(128)S(1)} %log.6, f32[64,128]{1,0:T(8,128)S(1)} %convolution_multiply_fusion, f32[36,64,128]{2,0,1:T(8,128)S(1)} %fusion.2, f32[128,64,128]{2,1,0:T(8,128)S(1)} %fusion.72, f32[128]{0:T(128)S(1)} %iota_multiply_fusion), kind=kOutput, calls=%fused_computation.79 | convolution fusion | flops 454173632 | bytes 6587648 | tf_op jit(solution)/shard_map/mnk,mj->jnk/dot_general | solution.py:48
  117.9 1.0 fusion.17
  118.9 3.9 %fusion.24 = bf16[128,64,128]{2,0,1:T(8,128)(2,1)S(1)} fusion(f32[128]{0:T(128)S(1)} %iota_multiply_fusion, f32[36,64,128]{2,0,1:T(8,128)S(1)} %get-tuple-element.5, f32[64]{0:T(128)S(1)} %fusion.17, f32[64]{0:T(128)S(1)} %get-tuple-element.4), kind=kOutput, calls=%fused_computation.34 | convolution fusion | flops 453583872 | bytes 3277824 | tf_op jit(solution)/shard_map/jnk,mj->mnk/dot_general | solution.py:65
  122.8 3.9 %fusion.21 = bf16[128,64,128]{2,0,1:T(8,128)(2,1)S(1)} fusion(f32[128]{0:T(128)S(1)} %iota_multiply_fusion, f32[36,64,128]{2,0,1:T(8,128)S(1)} %get-tuple-element.5, f32[64]{0:T(128)S(1)} %fusion.17, f32[64]{0:T(128)S(1)} %get-tuple-element.4), kind=kOutput, calls=%fused_computation.31 | convolution fusion | flops 453583872 | bytes 3277824 | tf_op jit(solution)/shard_map/jnk,mj->mnk/dot_general | solution.py:68
  126.7 2.0 fusion.6
  128.7 6.8 %convolution_subtract_fusion = f32[128,128,128]{2,1,0:T(8,128)} fusion(f32[128,128,128]{2,1,0:T(8,128)S(1)} %fusion.6, bf16[128,64,128]{2,0,1:T(8,128)(2,1)S(1)} %fusion.21, bf16[64,128,64]{2,0,1:T(8,128)(2,1)S(1)} %copy-done.1, bf16[64,128,64]{2,0,1:T(8,128)(2,1)S(1)} %copy-done), kind=kOutput, calls=%fused_computation.11 | convolution fusion | flops 274726912 | bytes 20971520 | tf_op jit(solution)/shard_map/mnk,nmq->mkq/dot_general | solution.py:76
  135.4 0.4 fusion.67
  136.1 78.1 %psum.7 = f32[32,128]{1,0:T(8,128)S(1)} all-reduce(f32[32,128]{1,0:T(8,128)S(1)} %fusion.19), channel_id=1, replica_groups=mesh['groups'=2,'dp'=16] {'dp'}, use_global_device_ids=true, to_apply=%region_5.0 | all-reduce | flops 4096 | bytes 32768 | tf_op jit(solution)/shard_map/psum | solution.py:62
  214.2 0.4 convolution_add_fusion
  214.7 0.5 log_add_fusion
  215.3 39.1 %reduce-scatter.2.cloned.1.call-done = f32[8,128,128]{2,1,0:T(8,128)} async-done(((f32[128,128,128]{2,1,0:T(8,128)}), f32[8,128,128]{2,1,0:T(8,128)}) %reduce-scatter.2.cloned.1.call-update) | async-done | bytes 524304 | tf_op jit(solution)/shard_map/reduce_scatter | solution.py:74
  254.3 1.9 broadcast_divide_fusion
  (24 shorter events, 1.0 us)
Async XLA Ops:
  11.3 7.7 %copy-start.3 = (f32[128]{0:T(128)S(1)}, f32[128]{0:T(128)}, u32[]{:S(2)}) copy-start(f32[128]{0:T(128)} %param.10) | copy-start | bytes 1540
  11.3 7.7 %copy-start.4 = (f32[32]{0:T(128)S(1)}, f32[32]{0:T(128)}, u32[]{:S(2)}) copy-start(f32[32]{0:T(128)} %param.9) | copy-start | bytes 388
  11.3 7.7 %copy-start.2 = (f32[64]{0:T(128)S(1)}, f32[64]{0:T(128)}, u32[]{:S(2)}) copy-start(f32[64]{0:T(128)} %param.11) | copy-start | bytes 772
  11.3 7.9 %copy-start.5 = (s32[64]{0:T(128)S(1)}, s32[64]{0:T(128)}, u32[]{:S(2)}) copy-start(s32[64]{0:T(128)} %param.8) | copy-start | bytes 772
  11.3 85.1 %all-to-all-start = ((bf16[16,8,128,128]{2,3,1,0:T(8,128)(2,1)}), bf16[16,8,128,128]{2,3,1,0:T(8,128)(2,1)}, u32[]{:S(2)}, u32[]{:S(2)}) async-start(bf16[16,8,128,128]{2,3,1,0:T(8,128)(2,1)} %stack.2), calls=%async_computation | async-start | bytes 8388608 | tf_op jit(solution)/shard_map/all_to_all | solution.py:36
  18.9 235.4 %reduce-scatter.2.cloned.1.call-start = ((), (), s32[]{:S(2)}) async-start(), calls=%async_computation.2 | async-start | bytes 8912896 | tf_op jit(solution)/shard_map/reduce_scatter | solution.py:74
  100.9 3.6 %copy-start = (bf16[64,128,64]{2,0,1:T(8,128)(2,1)S(1)}, bf16[64,128,64]{2,0,1:T(8,128)(2,1)}, u32[]{:S(2)}) copy-start(bf16[64,128,64]{2,0,1:T(8,128)(2,1)} %get-tuple-element.2) | copy-start | bytes 3145732
  100.9 3.6 %copy-start.1 = (bf16[64,128,64]{2,0,1:T(8,128)(2,1)S(1)}, bf16[64,128,64]{2,0,1:T(8,128)(2,1)}, u32[]{:S(2)}) copy-start(bf16[64,128,64]{2,0,1:T(8,128)(2,1)} %get-tuple-element.3) | copy-start | bytes 3145732
Sparse Core Ops, SparseCore 0:
  135.6 118.7 reduce-scatter.1
